TPU v7x, 256 devices: a whole 4x4x8 slice. The times are simulated.
256 devices in a mesh: seq: 64 (over y, z, core), tp: 4 (over x).
Axes of the slice: x: 4, y: 4, z: 8, core: 2. Of those that a mesh axis runs over, the one named last changes fastest.
Arguments:
- stream: bfloat16 [8192, 2048], P('seq'), may hold values from -256 to 256
- lengths: int32 [6], replicated, may hold values from 1 to 7168, 8192 in all
- q_weight: bfloat16 [2048, 1536], P(None, 'tp'), may hold values from -0.125 to 0.125
- kv_down: bfloat16 [2048, 576], replicated, may hold values from -0.125 to 0.125
- latent_gain: float32 [512], replicated, may hold values from 0.1 to 1.9
- kv_up: bfloat16 [8, 512, 256], P('tp'), may hold values from -0.25 to 0.25
- out_weight: bfloat16 [1024, 2048], P('tp'), may hold values from -0.1875 to 0.1875
- moe_gain: float32 [2048], replicated, may hold values from 0.1 to 1.9
- routes: int32 [8192, 6], P('seq'), may hold values from 0 to 63, all different within a row; in each aligned block of 128 rows (0 to 127, 128 to 255, ...) at most 24 rows name the same one
- route_weight: float32 [8192, 6], P('seq'), may hold values from 0.05 to 0.5
- expert_gate: bfloat16 [64, 2048, 1408], P('seq', None, 'tp'), may hold values from -0.125 to 0.125
- expert_up: bfloat16 [64, 2048, 1408], P('seq', None, 'tp'), may hold values from -0.125 to 0.125
- expert_down: bfloat16 [64, 1408, 2048], P('seq', 'tp'), may hold values from -0.15625 to 0.15625
Outputs:
- layer_out: bfloat16 [8192, 2048], P('seq')
- latent_cache: bfloat16 [8192, 576], P('seq')
Inputs may be any that keep to these rules, and one draw needn't show every extreme that they name: 6 lengths summing to 8192, the longest exactly 7168. In each aligned block of 128 rows no expert is named by more than 24 routes, a bound that some block reaches.
All inputs are finite; a program needn't handle non-finite values.
Results may differ from a plain program's by a relative error of at most 0.0075.
Values may be sent and summed in bfloat16 or wider, within the bound.
A program may use at most 128 MiB of HBM per device.

v0:
```python
import jax
import jax.numpy as jnp
from jax import lax
from jax.sharding import PartitionSpec as P

D = 2048
NOPE = 128
ROPE = 64
LATENT = 512
VDIM = 128
THETA = 50000.0


def place(token_index, lengths):
    prompt_ends = jnp.cumsum(lengths)
    before = (prompt_ends[None, :] <= token_index[:, None]).astype(jnp.int32)
    segment = jnp.sum(before, axis=1)
    prompt_start = jnp.sum(before * lengths[None, :], axis=1)
    return (segment, token_index - prompt_start)


def angles(position):
    half_rope = ROPE // 2
    frequency = THETA ** (-2.0 * jnp.arange(half_rope, dtype=jnp.float32) / ROPE)
    angle_table = position.astype(jnp.float32)[:, None] * frequency[None, :]
    return (jnp.cos(angle_table), jnp.sin(angle_table))


def rotate(values, cos_table, sin_table):
    half_rope = ROPE // 2
    first_half = values[..., :half_rope]
    second = values[..., half_rope:]
    return jnp.concatenate(
        [first_half * cos_table - second * sin_table, first_half * sin_table + second * cos_table],
        axis=-1,
    )


def on_device(
    stream,
    lengths,
    q_weight,
    kv_down,
    latent_gain,
    kv_up,
    out_weight,
    moe_gain,
    routes,
    route_weight,
    expert_gate,
    expert_up,
    expert_down,
):
    tok_count = stream.shape[0]
    head_count = kv_up.shape[0]
    first_row = lax.axis_index("seq") * tok_count
    token_index = first_row + jnp.arange(tok_count, dtype=jnp.int32)
    segment, position = place(token_index, lengths)
    cos_table, sin_table = angles(position)
    kv_proj = jnp.dot(stream, kv_down, preferred_element_type=jnp.float32)
    compressed = kv_proj[:, :LATENT]
    factor = lax.rsqrt(jnp.mean(compressed * compressed, axis=1, keepdims=True) + 1e-06)
    latent = jnp.concatenate(
        [
            compressed * factor * latent_gain[None, :],
            rotate(kv_proj[:, LATENT:], cos_table, sin_table),
        ],
        axis=1,
    ).astype(jnp.bfloat16)
    q_proj = jnp.dot(stream, q_weight, preferred_element_type=jnp.float32).astype(jnp.bfloat16)
    q_proj = q_proj.reshape(tok_count, head_count, NOPE + ROPE)
    absorbed = jnp.einsum(
        "thj,hcj->thc", q_proj[:, :, :NOPE], kv_up[:, :, :NOPE], preferred_element_type=jnp.float32
    )
    rotated = rotate(
        q_proj[:, :, NOPE:].astype(jnp.float32), cos_table[:, None, :], sin_table[:, None, :]
    )
    softmax_scale = (NOPE + ROPE) ** (-0.5)
    queries = (jnp.concatenate([absorbed, rotated], axis=2) * softmax_scale).astype(jnp.bfloat16)
    queries = queries.reshape(tok_count * head_count, LATENT + ROPE)
    row_segment = jnp.repeat(segment, head_count)
    row_index = jnp.repeat(token_index, head_count)
    row_total = tok_count * head_count
    shard_rows = lax.all_gather(latent, "seq", axis=0, tiled=True)
    key_count = shard_rows.shape[0]
    key_index = jnp.arange(key_count, dtype=jnp.int32)
    key_segment, unused = place(key_index, lengths)
    allowed = (row_segment[:, None] == key_segment[None, :]) & (
        key_index[None, :] <= row_index[:, None]
    )
    running_max = jnp.full((row_total,), -1e30, jnp.float32)
    scores = jnp.einsum("ra,ka->rk", queries, shard_rows, preferred_element_type=jnp.float32)
    block_peak = jnp.max(jnp.where(allowed, scores, -jnp.inf), axis=1)
    new_peak = jnp.maximum(running_max, block_peak)
    weights = jnp.where(allowed, jnp.exp(scores - new_peak[:, None]), 0.0)
    running_sum = jnp.sum(weights, axis=1)
    context_sum = jnp.dot(
        weights.astype(jnp.bfloat16), shard_rows[:, :LATENT], preferred_element_type=jnp.float32
    )
    running_max, running_sum, context_sum = (new_peak, running_sum, context_sum)
    context = (context_sum / running_sum[:, None]).reshape(tok_count, head_count, LATENT)
    heads_out = jnp.einsum(
        "thc,hcv->thv",
        context,
        kv_up[:, :, NOPE:].astype(jnp.float32),
        precision=lax.Precision.HIGHEST,
    )
    heads_out = heads_out.astype(jnp.bfloat16).reshape(tok_count, head_count * VDIM)
    partial_attention = jnp.dot(heads_out, out_weight, preferred_element_type=jnp.float32)
    tp_count = lax.axis_size("tp")
    col_width = D // tp_count
    col_start = lax.axis_index("tp") * col_width
    attention_pieces = partial_attention.astype(jnp.bfloat16).reshape(
        tok_count, tp_count, col_width
    )
    attention_pieces = lax.all_to_all(
        attention_pieces.transpose(1, 0, 2), "tp", split_axis=0, concat_axis=0, tiled=True
    )
    attention_part = jnp.sum(attention_pieces.astype(jnp.float32), axis=0)
    stream_part = lax.dynamic_slice_in_dim(stream, col_start, col_width, 1)
    hidden = stream_part.astype(jnp.float32) + attention_part
    normed = hidden.astype(jnp.bfloat16)
    experts = lax.axis_size("seq")
    top_k = routes.shape[1]
    capacity = min(tok_count, max(2, 2 * tok_count * top_k // experts))
    flat_routes = routes.reshape(-1)
    onehot = (flat_routes[:, None] == jnp.arange(experts, dtype=jnp.int32)[None, :]).astype(
        jnp.int32
    )
    slot_rank = jnp.sum((jnp.cumsum(onehot, axis=0) - onehot) * onehot, axis=1)
    slot_index = flat_routes * capacity + slot_rank
    slot_table = (
        slot_index[:, None] == jnp.arange(experts * capacity, dtype=jnp.int32)[None, :]
    ).astype(jnp.bfloat16)
    placing = jnp.sum(slot_table.reshape(tok_count, top_k, experts * capacity), axis=1)
    outgoing = jnp.einsum("ts,td->sd", placing, normed, preferred_element_type=jnp.float32).astype(
        jnp.bfloat16
    )
    outgoing = outgoing.reshape(experts, capacity, col_width)
    chunk_count = 2
    chunk_slots = capacity // chunk_count
    returned_chunks = []
    for chunk in range(chunk_count):
        sending = outgoing[:, chunk * chunk_slots : (chunk + 1) * chunk_slots]
        received = lax.all_to_all(sending, "seq", split_axis=0, concat_axis=0, tiled=True)
        sources, slot_count, _ = received.shape
        flat_part = received.reshape(sources * slot_count, col_width)
        flat_rows = lax.all_gather(flat_part, "tp", axis=1, tiled=True).astype(jnp.float32)
        flat_rows = (
            flat_rows
            * lax.rsqrt(jnp.mean(flat_rows * flat_rows, axis=1, keepdims=True) + 1e-06)
            * moe_gain[None, :]
        ).astype(jnp.bfloat16)
        gate_act = jnp.dot(flat_rows, expert_gate[0], preferred_element_type=jnp.float32)
        up_act = jnp.dot(flat_rows, expert_up[0], preferred_element_type=jnp.float32)
        hidden_units = (jax.nn.silu(gate_act) * up_act).astype(jnp.bfloat16)
        expert_out = jnp.dot(
            hidden_units, expert_down[0], preferred_element_type=jnp.float32
        ).astype(jnp.bfloat16)
        expert_sum = lax.psum_scatter(expert_out, "tp", scatter_dimension=1, tiled=True)
        expert_sum = expert_sum.reshape(sources, slot_count, col_width)
        returned_chunks.append(
            lax.all_to_all(expert_sum, "seq", split_axis=0, concat_axis=0, tiled=True)
        )
    returned = jnp.concatenate(returned_chunks, axis=1)
    gathered = returned.reshape(experts * capacity, col_width)[slot_index].reshape(
        tok_count, top_k, col_width
    )
    moe = jnp.zeros((tok_count, col_width), jnp.float32)
    for route_slot in range(top_k):
        moe = moe + route_weight[:, route_slot][:, None] * gathered[:, route_slot].astype(
            jnp.float32
        )
    layer_part = (hidden + moe).astype(jnp.bfloat16)
    repeated_part = jnp.broadcast_to(layer_part[None], (tp_count,) + layer_part.shape)
    layer_pieces = lax.all_to_all(repeated_part, "tp", split_axis=0, concat_axis=0, tiled=True)
    layer_out = layer_pieces.transpose(1, 0, 2).reshape(tok_count, D)
    return (layer_out, latent)


def solution(mesh):
    return jax.shard_map(
        on_device,
        mesh=mesh,
        in_specs=(
            P("seq", None),
            P(),
            P(None, "tp"),
            P(),
            P(),
            P("tp", None, None),
            P("tp", None),
            P(),
            P("seq", None),
            P("seq", None),
            P("seq", None, "tp"),
            P("seq", None, "tp"),
            P("seq", "tp", None),
        ),
        out_specs=(P("seq", None), P("seq", None)),
        check_vma=False,
    )
```

profile of v0, /device:TPU:1, one launch (start us, length us, event | category | flops | bytes accessed | tf_op | source)
XLA Modules:
  0.0 411.8 jit_solution(14239379274214092569)
XLA Ops:
  7.3 1.0 reduce-window.18
  8.3 0.7 fusion.82
  9.1 1.9 fusion.94
  11.0 0.1 multiply_cosine_fusion
  11.2 0.1 multiply_convert_fusion
  11.3 0.7 pad_maximum_fusion.1
  12.2 0.1 eq.62
  12.3 0.1 eq.58
  12.4 1.8 convolution_convert_fusion.4
  14.3 0.1 copy.93
  14.4 0.1 copy.96
  14.6 0.1 copy.97
  14.8 0.2 eq.54
  15.0 0.2 le.48
  15.2 0.3 convolution_bitcast_fusion
  15.4 0.4 copy.95
  15.8 0.4 concatenate.17
  16.2 1.8 reduce-window.19
  18.0 0.3 slice_reduce_fusion
  18.3 0.1 fusion.76
  18.5 0.1 reduce_sum.104
  18.6 0.2 convert_reduce_fusion.1
  18.8 84.7 %all-gather.4.cloned.1.call-done = bf16[8192,576]{0,1:T(8,128)(2,1)} async-done(((bf16[128,576]{0,1:T(8,128)(2,1)}), bf16[8192,576]{0,1:T(8,128)(2,1)}) %all-gather.4.cloned.1.call-update) | async-done | bytes 9437200 | tf_op jit(solution)/shard_map/all_gather | solution.py:84
  103.5 6.8 %select_reduce_fusion = (f32[256]{0:T(256)S(1)}, f32[256,8192]{1,0:T(8,128)S(1)}) fusion(s32[256]{0:T(256)S(1)} %le.48, s32[8192]{0:T(1024)S(1)} %convert_reduce_fusion.1, s32[256]{0:T(256)S(1)} %eq.54, bf16[8192,576]{0,1:T(8,128)(2,1)} %all-gather.4.cloned.1.call-done, f32[256,32]{1,0:T(8,128)S(1)} %bitcast.130, f32[256,32]{1,0:T(8,128)S(1)} %bitcast.129, ...), kind=kOutput, calls=%fused_computation.4 | convolution fusion | flops 2426994432 | bytes 18451456 | tf_op jit(solution)/shard_map/ra,ka->rk/dot_general | solution.py:92
  110.3 2.8 fusion.9
  113.1 6.3 %fusion.41 = f32[256,512]{1,0:T(8,128)S(1)} fusion(bf16[8192,576]{0,1:T(8,128)(2,1)} %all-gather.4.cloned.1.call-done, f32[256,8192]{1,0:T(8,128)S(1)} %get-tuple-element.33, f32[256]{0:T(256)S(1)} %broadcast_maximum_fusion, s32[256]{0:T(256)S(1)} %le.48, s32[8192]{0:T(1024)S(1)} %convert_reduce_fusion.1, s32[256]{0:T(256)S(1)} %eq.54, f32[256]{0:T(256)S(1)} %fusion.9), kind=kOutput, calls=%fused_computation.49 | convolution fusion | flops 2160197632 | bytes 17338368 | tf_op jit(solution)/shard_map/dot_general | solution.py:97
  119.5 0.3 reshape.240
  119.8 0.5 convolution_convert_fusion.5
  120.3 0.3 convolution_convert_fusion.3
  120.6 0.8 copy.143
  121.5 4.0 all-to-all-start
  125.5 0.7 fusion.18
  126.2 8.2 %all-to-all-done = bf16[4,128,512]{2,1,0:T(8,128)(2,1)S(1)} async-done(((bf16[4,128,512]{2,1,0:T(8,128)(2,1)}), bf16[4,128,512]{2,1,0:T(8,128)(2,1)S(1)}, u32[]{:S(2)}, u32[]{:S(2)}) %all-to-all-start) | async-done | bytes 524320 | tf_op jit(solution)/shard_map/all_to_all | solution.py:116
  134.5 0.6 convolution_convert_fusion.2
  135.2 0.5 fusion.92
  135.7 39.2 %all_to_all.30 = bf16[64,12,512]{2,1,0:T(8,128)(2,1)S(1)} all-to-all(bf16[64,12,512]{2,1,0:T(8,128)(2,1)S(1)} %get-tuple-element.8), channel_id=1, replica_groups=mesh['seq'=64,'tp'=4] {'seq'}, dimensions={0} | all-to-all | bytes 1572864 | tf_op jit(solution)/shard_map/all_to_all | solution.py:145
  174.9 1.1 reshape.245
  176.0 34.5 %all_to_all.31 = bf16[64,12,512]{2,1,0:T(8,128)(2,1)S(1)} all-to-all(bf16[64,12,512]{2,1,0:T(8,128)(2,1)S(1)} %get-tuple-element.9), channel_id=1, replica_groups=mesh['seq'=64,'tp'=4] {'seq'}, dimensions={0} | all-to-all | bytes 1572864 | tf_op jit(solution)/shard_map/all_to_all | solution.py:145
  210.6 1.1 reshape.247
  211.8 1.2 all-gather.6.cloned.1.call-done
  213.0 2.7 fusion.3
  215.8 3.8 fusion.27
  219.6 7.6 %convolution_convert_fusion.1 = bf16[768,2048]{1,0:T(8,128)(2,1)} fusion(bf16[1,352,2048]{2,1,0:T(8,128)(2,1)} %param.25, bf16[1,2048,352]{1,2,0:T(8,128)(2,1)} %param.24, f32[768,352]{0,1:T(8,128)} %fusion.27, bf16[768,2048]{1,0:T(8,128)(2,1)S(1)} %copy-done.4, f32[2048]{0:T(1024)S(1)} %copy-done.12, f32[768]{0:T(1024)S(1)} %add_rsqrt_fusion.1), kind=kOutput, calls=%fused_computation.27 | convolution fusion | flops 2224078848 | bytes 10267648 | tf_op jit(solution)/shard_map/dot_general | solution.py:157
  227.2 0.3 reduce-scatter.5.cloned.1.call-start
  227.5 29.6 %all-gather.8.cloned.1.call-done = bf16[768,2048]{1,0:T(8,128)(2,1)} async-done(((bf16[768,512]{1,0:T(8,128)(2,1)}), bf16[768,2048]{1,0:T(8,128)(2,1)}) %all-gather.8.cloned.1.call-update) | async-done | bytes 3145744 | tf_op jit(solution)/shard_map/all_gather | solution.py:148
  257.1 2.7 fusion.6
  259.9 3.8 fusion.25
  263.7 7.6 %convolution_convert_fusion = bf16[768,2048]{1,0:T(8,128)(2,1)} fusion(bf16[1,352,2048]{2,1,0:T(8,128)(2,1)} %param.25, bf16[1,2048,352]{1,2,0:T(8,128)(2,1)} %param.24, f32[768,352]{0,1:T(8,128)} %fusion.25, bf16[768,2048]{1,0:T(8,128)(2,1)S(1)} %copy-done.3, f32[768]{0:T(1024)S(1)} %add_rsqrt_fusion, f32[2048]{0:T(1024)S(1)} %copy-done.12), kind=kOutput, calls=%fused_computation.26 | convolution fusion | flops 2224078848 | bytes 10267648 | tf_op jit(solution)/shard_map/dot_general | solution.py:157
  271.3 29.3 %reduce-scatter.3.cloned.1.call-done = bf16[768,512]{1,0:T(8,128)(2,1)} async-done(((bf16[768,2048]{1,0:T(8,128)(2,1)}), bf16[768,512]{1,0:T(8,128)(2,1)}) %reduce-scatter.3.cloned.1.call-update) | async-done | bytes 786448 | tf_op jit(solution)/shard_map/reduce_scatter | solution.py:160
  300.6 2.1 reshape.246
  302.8 10.9 %all-to-all-start.2 = ((bf16[64,12,512]{2,1,0:T(8,128)(2,1)}), bf16[64,12,512]{2,1,0:T(8,128)(2,1)S(1)}, u32[]{:S(2)}, u32[]{:S(2)}) async-start(bf16[64,12,512]{2,1,0:T(8,128)(2,1)} %reshape.246), calls=%async_computation.3 | async-start | bytes 2097152 | tf_op jit(solution)/shard_map/all_to_all | solution.py:163
  313.6 30.0 %reduce-scatter.5.cloned.1.call-done = bf16[768,512]{1,0:T(8,128)(2,1)} async-done(((bf16[768,2048]{1,0:T(8,128)(2,1)}), bf16[768,512]{1,0:T(8,128)(2,1)}) %reduce-scatter.5.cloned.1.call-update) | async-done | bytes 786448 | tf_op jit(solution)/shard_map/reduce_scatter | solution.py:160
  343.7 2.2 reshape.248
  345.8 10.9 %all-to-all-start.4 = ((bf16[64,12,512]{2,1,0:T(8,128)(2,1)}), bf16[64,12,512]{2,1,0:T(8,128)(2,1)}, u32[]{:S(2)}, u32[]{:S(2)}) async-start(bf16[64,12,512]{2,1,0:T(8,128)(2,1)} %reshape.248), calls=%async_computation.6 | async-start | bytes 2097152 | tf_op jit(solution)/shard_map/all_to_all | solution.py:163
  356.8 0.1 mul.276
  357.0 28.2 %all-to-all-done.4 = bf16[64,12,512]{2,1,0:T(8,128)(2,1)} async-done(((bf16[64,12,512]{2,1,0:T(8,128)(2,1)}), bf16[64,12,512]{2,1,0:T(8,128)(2,1)}, u32[]{:S(2)}, u32[]{:S(2)}) %all-to-all-start.4) | async-done | bytes 786464 | tf_op jit(solution)/shard_map/all_to_all | solution.py:163
  385.2 1.7 pad_maximum_fusion
  386.9 2.7 gather_fusion
  389.6 0.3 reshape.250
  389.9 1.1 fusion.93
  391.0 1.1 fusion.67
  392.2 11.7 %all_to_all.32 = bf16[4,128,512]{2,1,0:T(8,128)(2,1)S(1)} all-to-all(bf16[4,128,512]{2,1,0:T(8,128)(2,1)S(1)} %broadcast_in_dim.20), channel_id=1, replica_groups=mesh['seq'=64,'tp'=4] {'tp'}, dimensions={0} | all-to-all | bytes 1048576 | tf_op jit(solution)/shard_map/all_to_all | solution.py:176
  403.9 0.3 copy.111
  404.2 1.0 copy.112
  (58 shorter events, 1.2 us)
Async XLA Ops:
  7.2 1.9 copy-start
  7.2 5.2 %copy-start.2 = (bf16[128,2048]{1,0:T(8,128)(2,1)S(1)}, bf16[128,2048]{1,0:T(8,128)(2,1)}, u32[]{:S(2)}) copy-start(bf16[128,2048]{1,0:T(8,128)(2,1)} %param.13) | copy-start | bytes 1572868
  7.2 4.0 copy-start.11
  7.2 4.8 %copy-start.9 = (s32[128,6]{0,1:T(8,128)S(1)}, s32[128,6]{0,1:T(8,128)}, u32[]{:S(2)}) copy-start(s32[128,6]{0,1:T(8,128)} %param.21) | copy-start | bytes 9220
  7.2 96.3 %all-gather.4.cloned.1.call-start = ((), (), s32[]{:S(2)}) async-start(), calls=%async_computation.8 | async-start | bytes 9584640 | tf_op jit(solution)/shard_map/all_gather | solution.py:84
  9.0 6.1 %copy-start.8 = (bf16[2,512,256]{2,1,0:T(8,128)(2,1)S(1)}, bf16[2,512,256]{2,1,0:T(8,128)(2,1)}, u32[]{:S(2)}) copy-start(bf16[2,512,256]{2,1,0:T(8,128)(2,1)} %param.18) | copy-start | bytes 1572868
  113.1 7.2 %copy-start.7 = (bf16[256,2048]{1,0:T(8,128)(2,1)S(1)}, bf16[256,2048]{1,0:T(8,128)(2,1)}, u32[]{:S(2)}) copy-start(bf16[256,2048]{1,0:T(8,128)(2,1)} %param.19) | copy-start | bytes 3145732
  121.5 13.0 %all-to-all-start = ((bf16[4,128,512]{2,1,0:T(8,128)(2,1)}), bf16[4,128,512]{2,1,0:T(8,128)(2,1)S(1)}, u32[]{:S(2)}, u32[]{:S(2)}) async-start(bf16[4,128,512]{2,1,0:T(8,128)(2,1)} %bitcast.120), calls=%async_computation | async-start | bytes 1048576 | tf_op jit(solution)/shard_map/all_to_all | solution.py:116
  125.4 87.6 %all-gather.6.cloned.1.call-start = ((), (), s32[]{:S(2)}) async-start(), calls=%async_computation.9 | async-start | bytes 3932160 | tf_op jit(solution)/shard_map/all_gather | solution.py:148
  134.5 0.7 copy-start.5
  176.0 81.1 %all-gather.8.cloned.1.call-start = ((), (), s32[]{:S(2)}) async-start(), calls=%async_computation.11 | async-start | bytes 3932160 | tf_op jit(solution)/shard_map/all_gather | solution.py:148
  210.6 5.2 %copy-start.12 = (f32[2048]{0:T(1024)S(1)}, f32[2048]{0:T(1024)}, u32[]{:S(2)}) copy-start(f32[2048]{0:T(1024)} %param.20) | copy-start | bytes 24580
  211.7 88.9 %reduce-scatter.3.cloned.1.call-start = ((), (), s32[]{:S(2)}) async-start(), calls=%async_computation.10 | async-start | bytes 3932160 | tf_op jit(solution)/shard_map/reduce_scatter | solution.py:160
  213.0 2.8 copy-start.4
  227.2 116.4 %reduce-scatter.5.cloned.1.call-start = ((), (), s32[]{:S(2)}) async-start(), calls=%async_computation.12 | async-start | bytes 3932160 | tf_op jit(solution)/shard_map/reduce_scatter | solution.py:160
  257.1 2.8 copy-start.3
  302.8 54.2 %copy-start.10 = (f32[128,6]{0,1:T(8,128)S(1)}, f32[128,6]{0,1:T(8,128)}, u32[]{:S(2)}) copy-start(f32[128,6]{0,1:T(8,128)} %param.22) | copy-start | bytes 9220
  302.8 43.1 %all-to-all-start.2 = ((bf16[64,12,512]{2,1,0:T(8,128)(2,1)}), bf16[64,12,512]{2,1,0:T(8,128)(2,1)S(1)}, u32[]{:S(2)}, u32[]{:S(2)}) async-start(bf16[64,12,512]{2,1,0:T(8,128)(2,1)} %reshape.246), calls=%async_computation.3 | async-start | bytes 2097152 | tf_op jit(solution)/shard_map/all_to_all | solution.py:163
  345.8 39.4 %all-to-all-start.4 = ((bf16[64,12,512]{2,1,0:T(8,128)(2,1)}), bf16[64,12,512]{2,1,0:T(8,128)(2,1)}, u32[]{:S(2)}, u32[]{:S(2)}) async-start(bf16[64,12,512]{2,1,0:T(8,128)(2,1)} %reshape.248), calls=%async_computation.6 | async-start | bytes 2097152 | tf_op jit(solution)/shard_map/all_to_all | solution.py:163
  389.9 1.2 copy-start.6
  389.9 15.3 %copy-start.1 = (bf16[2048,576]{0,1:T(8,128)(2,1)S(1)}, bf16[2048,576]{0,1:T(8,128)(2,1)}, u32[]{:S(2)}) copy-start(bf16[2048,576]{0,1:T(8,128)(2,1)} %param.16) | copy-start | bytes 7077892
Sparse Core Ops, SparseCore 0:
  12.1 91.3 all-gather.3
  176.1 36.8 all-gather.5
  214.8 42.2 all-gather.7
  259.5 41.1 reduce-scatter.2
  303.0 40.5 reduce-scatter.4
where the time goes:
time: 412 us
  waiting for transfers between devices  211 us (51%)
  blocking collectives  85.4 us (21%)
  matrix products  41.3 us (10%)
  starting transfers between devices  26.2 us (6%)
  other arithmetic  18 us (4%)
  local copies, waits for them, and re-layouts  15.3 us (4%)
  between operations  14.2 us (3%)
    all_gather x1, waiting for transfers between devices, on_device(): shard_rows = lax.all_gather(latent, 'seq', axis=0, tiled=True)  84.7 us
    all_to_all x2, blocking collectives, on_device(): lax.all_to_all(sending, 'seq', split_axis=0, concat_axis=0, tiled=True)  73.7 us
    reduce_scatter x2, waiting for transfers between devices, on_device(): lax.psum_scatter(expert_out, 'tp', scatter_dimension=1, tiled=True)  59.3 us
    all_gather x2, waiting for transfers between devices, on_device(): lax.all_gather(flat_part, 'tp', axis=1, tiled=True).astype(jnp.float32)  30.8 us
    all_to_all x2, waiting for transfers between devices, on_device(): lax.all_to_all(expert_sum, 'seq', split_axis=0, concat_axis=0, tiled=True)  28.2 us
    all_to_all x2, starting transfers between devices, on_device(): lax.all_to_all(expert_sum, 'seq', split_axis=0, concat_axis=0, tiled=True)  21.8 us
    dot_general x2, matrix products, on_device(): jnp.dot(hidden_units, expert_down[0], preferred_element_type=jnp.float32)  15.2 us
    all_to_all x1, blocking collectives, on_device(): lax.all_to_all(repeated_part, 'tp', split_axis=0, concat_axis=0, tiled=True)  11.7 us
  transfers between devices with their start and end apart: 8, of which 7 were waited for; matrix products, arithmetic and copies ran while one was open for 10% of the time, Pallas kernels for 0%

commit v1 on v0

--- a/solution.py
+++ b/solution.py
@@ -81,7 +81,15 @@
     row_segment = jnp.repeat(segment, head_count)
     row_index = jnp.repeat(token_index, head_count)
     row_total = tok_count * head_count
-    shard_rows = lax.all_gather(latent, "seq", axis=0, tiled=True)
+    shard_rows = jnp.concatenate(
+        lax.all_to_all(
+            jnp.stack([latent for _ in range(lax.psum(1, "seq"))], axis=0),
+            "seq",
+            split_axis=0,
+            concat_axis=0,
+        ),
+        axis=0,
+    )
     key_count = shard_rows.shape[0]
     key_index = jnp.arange(key_count, dtype=jnp.int32)
     key_segment, unused = place(key_index, lengths)

time: 412 us -> 558 us (1.35)
  waiting for transfers between devices: 211 us -> 330 us
  local copies, waits for them, and re-layouts: 15.3 us -> 33.1 us
  starting transfers between devices: 26.2 us -> 39.7 us
    all_to_all x0 -> x1, waiting for transfers between devices: none -> 203 us  [on_device(): lax.all_to_all(jnp.stack([latent for _ in range(lax.psum(1, 'seq'))], axi...]
    all_gather x1 -> x0, waiting for transfers between devices: 84.7 us -> none  [on_device(): shard_rows = lax.all_gather(latent, 'seq', axis=0, tiled=True)]
    all_to_all x0 -> x1, starting transfers between devices: none -> 13.5 us  [on_device(): lax.all_to_all(jnp.stack([latent for _ in range(lax.psum(1, 'seq'))], axi...]
    reshape x0 -> x1, local copies, waits for them, and re-layouts: none -> 8.73 us  [on_device(): jnp.concatenate(lax.all_to_all(jnp.stack([latent for _ in range(lax.psum(...]
    another operation x0 -> x1, local copies, waits for them, and re-layouts: none -> 5.93 us  [on_device(): jnp.stack([latent for _ in range(lax.psum(1, 'seq'))], axis=0)]
  transfers between devices with their start and end apart: 8 -> 8, of which waited for: 7 -> 7; matrix products, arithmetic and copies ran while one was open for 10% -> 7% of each run, Pallas kernels for 0% -> 0%
where the time goes in v1:
time: 558 us; the launch traced here: 557 us
  waiting for transfers between devices  330 us (59%)
  blocking collectives  80.1 us (14%)
  matrix products  42 us (8%)
  starting transfers between devices  39.7 us (7%)
  local copies, waits for them, and re-layouts  33.1 us (6%)
  other arithmetic  17.3 us (3%)
  between operations  14.3 us (3%)
    all_to_all x1, waiting for transfers between devices, on_device(): lax.all_to_all(jnp.stack([latent for _ in range(lax.psum(1, 'seq'))], axi...  203 us
    all_to_all x2, blocking collectives, on_device(): lax.all_to_all(sending, 'seq', split_axis=0, concat_axis=0, tiled=True)  68.4 us
    reduce_scatter x2, waiting for transfers between devices, on_device(): lax.psum_scatter(expert_out, 'tp', scatter_dimension=1, tiled=True)  59.9 us
    all_gather x2, waiting for transfers between devices, on_device(): lax.all_gather(flat_part, 'tp', axis=1, tiled=True).astype(jnp.float32)  30.2 us
    all_to_all x2, waiting for transfers between devices, on_device(): lax.all_to_all(expert_sum, 'seq', split_axis=0, concat_axis=0, tiled=True)  28.2 us
    all_to_all x2, starting transfers between devices, on_device(): lax.all_to_all(expert_sum, 'seq', split_axis=0, concat_axis=0, tiled=True)  21.8 us
    dot_general x2, matrix products, on_device(): jnp.dot(hidden_units, expert_down[0], preferred_element_type=jnp.float32)  16.7 us
    all_to_all x1, starting transfers between devices, on_device(): lax.all_to_all(jnp.stack([latent for _ in range(lax.psum(1, 'seq'))], axi...  13.5 us
  transfers between devices with their start and end apart: 8, of which 7 were waited for; matrix products, arithmetic and copies ran while one was open for 7% of the time, Pallas kernels for 0%

profile of v1, /device:TPU:1, one launch (start us, length us, event | category | flops | bytes accessed | tf_op | source)
XLA Modules:
  0.0 556.8 jit_solution(14363406447608806796)
XLA Ops:
  7.2 1.0 reduce-window.18
  8.2 0.7 fusion.82
  9.0 1.8 fusion.94
  10.9 0.1 multiply_cosine_fusion
  11.1 0.1 multiply_convert_fusion
  11.2 5.9 %stack.2 = bf16[64,128,576]{1,2,0:T(8,128)(2,1)} broadcast(bf16[128,576]{0,1:T(8,128)(2,1)S(1)} %pad_maximum_fusion.1), dimensions={1,2} | broadcast | bytes 9584640 | tf_op jit(solution)/shard_map/stack | solution.py:86
  17.2 13.5 %all-to-all-start = ((bf16[64,128,576]{1,2,0:T(8,128)(2,1)}), bf16[64,128,576]{1,2,0:T(8,128)(2,1)}, u32[]{:S(2)}, u32[]{:S(2)}) async-start(bf16[64,128,576]{1,2,0:T(8,128)(2,1)} %stack.2), calls=%async_computation | async-start | bytes 18874368 | tf_op jit(solution)/shard_map/all_to_all | solution.py:85
  30.8 0.1 eq.62
  30.9 0.1 eq.58
  31.1 0.4 convolution_convert_fusion.4
  32.0 0.2 eq.54
  32.2 0.2 le.48
  32.4 0.3 convolution_bitcast_fusion
  32.6 0.4 copy.99
  33.1 0.4 concatenate.19
  33.5 1.8 reduce-window.19
  35.3 0.3 slice_reduce_fusion
  35.6 0.1 fusion.76
  35.7 0.1 reduce_sum.104
  35.8 0.2 convert_reduce_fusion.1
  36.0 202.9 %all-to-all-done = bf16[64,128,576]{1,2,0:T(8,128)(2,1)} async-done(((bf16[64,128,576]{1,2,0:T(8,128)(2,1)}), bf16[64,128,576]{1,2,0:T(8,128)(2,1)}, u32[]{:S(2)}, u32[]{:S(2)}) %all-to-all-start) | async-done | bytes 9437216 | tf_op jit(solution)/shard_map/all_to_all | solution.py:85
  238.9 6.7 %select_reduce_fusion = (f32[256]{0:T(256)S(1)}, f32[256,8192]{1,0:T(8,128)S(1)}) fusion(s32[256]{0:T(256)S(1)} %le.48, s32[8192]{0:T(1024)S(1)} %convert_reduce_fusion.1, s32[256]{0:T(256)S(1)} %eq.54, f32[256,32]{1,0:T(8,128)S(1)} %bitcast.140, f32[256,32]{1,0:T(8,128)S(1)} %bitcast.139, f32[256,512]{1,0:T(8,128)S(1)} %concatenate.19, ...), kind=kOutput, calls=%fused_computation.5 | convolution fusion | flops 2426994432 | bytes 18451456 | tf_op jit(solution)/shard_map/ra,ka->rk/dot_general | solution.py:100
  245.6 3.3 copy-done.2
  248.9 2.7 fusion.9
  251.7 8.7 %copy_bitcast_fusion = bf16[8192,576]{0,1:T(8,128)(2,1)} fusion(bf16[64,128,576]{1,2,0:T(8,128)(2,1)} %all-to-all-done), kind=kLoop, calls=%fused_computation.1 | loop fusion | bytes 18874368 | tf_op jit(solution)/shard_map/reshape | solution.py:84
  260.4 8.4 %fusion.41 = f32[256,512]{1,0:T(8,128)S(1)} fusion(bf16[8192,576]{0,1:T(8,128)(2,1)} %copy_bitcast_fusion, f32[256,8192]{1,0:T(8,128)} %copy-done.2, f32[256]{0:T(256)S(1)} %broadcast_maximum_fusion, s32[256]{0:T(256)S(1)} %le.48, s32[8192]{0:T(1024)S(1)} %convert_reduce_fusion.1, s32[256]{0:T(256)S(1)} %eq.54, f32[256]{0:T(256)S(1)} %fusion.9), kind=kOutput, calls=%fused_computation.50 | convolution fusion | flops 2160197632 | bytes 17338368 | tf_op jit(solution)/shard_map/dot_general | solution.py:105
  268.8 0.3 reshape.254
  269.1 0.5 convolution_convert_fusion.5
  269.6 0.3 convolution_convert_fusion.3
  269.9 0.8 copy.153
  270.8 4.0 all-to-all-start.1
  274.9 0.7 fusion.18
  275.6 9.1 %all-to-all-done.1 = bf16[4,128,512]{2,1,0:T(8,128)(2,1)S(1)} async-done(((bf16[4,128,512]{2,1,0:T(8,128)(2,1)}), bf16[4,128,512]{2,1,0:T(8,128)(2,1)S(1)}, u32[]{:S(2)}, u32[]{:S(2)}) %all-to-all-start.1) | async-done | bytes 524320 | tf_op jit(solution)/shard_map/all_to_all | solution.py:124
  284.8 0.6 convolution_convert_fusion.2
  285.4 0.5 fusion.92
  285.8 33.9 %all_to_all.35 = bf16[64,12,512]{2,1,0:T(8,128)(2,1)S(1)} all-to-all(bf16[64,12,512]{2,1,0:T(8,128)(2,1)S(1)} %get-tuple-element.8), channel_id=1, replica_groups=mesh['seq'=64,'tp'=4] {'seq'}, dimensions={0} | all-to-all | bytes 1572864 | tf_op jit(solution)/shard_map/all_to_all | solution.py:153
  319.8 1.1 reshape.259
  320.9 34.5 %all_to_all.36 = bf16[64,12,512]{2,1,0:T(8,128)(2,1)S(1)} all-to-all(bf16[64,12,512]{2,1,0:T(8,128)(2,1)S(1)} %get-tuple-element.9), channel_id=1, replica_groups=mesh['seq'=64,'tp'=4] {'seq'}, dimensions={0} | all-to-all | bytes 1572864 | tf_op jit(solution)/shard_map/all_to_all | solution.py:153
  355.4 1.0 reshape.261
  356.5 1.3 all-gather.3.cloned.1.call-done
  357.8 2.7 fusion.3
  360.7 3.9 fusion.27
  364.6 8.1 %convolution_convert_fusion.1 = bf16[768,2048]{1,0:T(8,128)(2,1)} fusion(bf16[1,352,2048]{2,1,0:T(8,128)(2,1)S(1)} %copy-done.16, bf16[1,2048,352]{1,2,0:T(8,128)(2,1)} %param.24, f32[768,352]{0,1:T(8,128)} %fusion.27, bf16[768,2048]{1,0:T(8,128)(2,1)} %all-gather.3.cloned.1.call-done, f32[2048]{0:T(1024)S(1)} %copy-done.17, f32[768]{0:T(1024)S(1)} %add_rsqrt_fusion.1), kind=kOutput, calls=%fused_computation.28 | convolution fusion | flops 2224078848 | bytes 10267648 | tf_op jit(solution)/shard_map/dot_general | solution.py:165
  372.7 0.3 reduce-scatter.5.cloned.1.call-start
  373.0 28.9 %all-gather.5.cloned.1.call-done = bf16[768,2048]{1,0:T(8,128)(2,1)} async-done(((bf16[768,512]{1,0:T(8,128)(2,1)}), bf16[768,2048]{1,0:T(8,128)(2,1)}) %all-gather.5.cloned.1.call-update) | async-done | bytes 3145744 | tf_op jit(solution)/shard_map/all_gather | solution.py:156
  401.9 2.7 fusion.6
  404.7 2.4 fusion.25
  407.1 8.6 %convolution_convert_fusion = bf16[768,2048]{1,0:T(8,128)(2,1)} fusion(bf16[1,352,2048]{2,1,0:T(8,128)(2,1)} %param.25, bf16[1,2048,352]{1,2,0:T(8,128)(2,1)} %param.24, f32[768,352]{0,1:T(8,128)} %fusion.25, bf16[768,2048]{1,0:T(8,128)(2,1)} %all-gather.5.cloned.1.call-done, f32[768]{0:T(1024)S(1)} %add_rsqrt_fusion, f32[2048]{0:T(1024)S(1)} %copy-done.17), kind=kOutput, calls=%fused_computation.27 | convolution fusion | flops 2224078848 | bytes 10267648 | tf_op jit(solution)/shard_map/dot_general | solution.py:165
  415.7 29.9 %reduce-scatter.3.cloned.1.call-done = bf16[768,512]{1,0:T(8,128)(2,1)} async-done(((bf16[768,2048]{1,0:T(8,128)(2,1)}), bf16[768,512]{1,0:T(8,128)(2,1)}) %reduce-scatter.3.cloned.1.call-update) | async-done | bytes 786448 | tf_op jit(solution)/shard_map/reduce_scatter | solution.py:168
  445.6 2.1 reshape.260
  447.8 10.9 %all-to-all-start.3 = ((bf16[64,12,512]{2,1,0:T(8,128)(2,1)}), bf16[64,12,512]{2,1,0:T(8,128)(2,1)S(1)}, u32[]{:S(2)}, u32[]{:S(2)}) async-start(bf16[64,12,512]{2,1,0:T(8,128)(2,1)} %reshape.260), calls=%async_computation.4 | async-start | bytes 2097152 | tf_op jit(solution)/shard_map/all_to_all | solution.py:171
  458.6 30.0 %reduce-scatter.5.cloned.1.call-done = bf16[768,512]{1,0:T(8,128)(2,1)} async-done(((bf16[768,2048]{1,0:T(8,128)(2,1)}), bf16[768,512]{1,0:T(8,128)(2,1)}) %reduce-scatter.5.cloned.1.call-update) | async-done | bytes 786448 | tf_op jit(solution)/shard_map/reduce_scatter | solution.py:168
  488.7 2.2 reshape.262
  490.8 10.9 %all-to-all-start.5 = ((bf16[64,12,512]{2,1,0:T(8,128)(2,1)}), bf16[64,12,512]{2,1,0:T(8,128)(2,1)}, u32[]{:S(2)}, u32[]{:S(2)}) async-start(bf16[64,12,512]{2,1,0:T(8,128)(2,1)} %reshape.262), calls=%async_computation.7 | async-start | bytes 2097152 | tf_op jit(solution)/shard_map/all_to_all | solution.py:171
  501.8 0.1 mul.276
  502.0 28.2 %all-to-all-done.5 = bf16[64,12,512]{2,1,0:T(8,128)(2,1)} async-done(((bf16[64,12,512]{2,1,0:T(8,128)(2,1)}), bf16[64,12,512]{2,1,0:T(8,128)(2,1)}, u32[]{:S(2)}, u32[]{:S(2)}) %all-to-all-start.5) | async-done | bytes 786464 | tf_op jit(solution)/shard_map/all_to_all | solution.py:171
  530.2 1.7 pad_maximum_fusion
  531.9 2.7 gather_fusion
  534.6 0.3 reshape.264
  534.9 1.1 fusion.93
  536.0 1.1 fusion.67
  537.2 11.7 %all_to_all.37 = bf16[4,128,512]{2,1,0:T(8,128)(2,1)S(1)} all-to-all(bf16[4,128,512]{2,1,0:T(8,128)(2,1)S(1)} %broadcast_in_dim.20), channel_id=1, replica_groups=mesh['seq'=64,'tp'=4] {'tp'}, dimensions={0} | all-to-all | bytes 1048576 | tf_op jit(solution)/shard_map/all_to_all | solution.py:184
  548.9 0.3 copy.116
  549.2 1.0 copy.117
  (69 shorter events, 1.4 us)
Async XLA Ops:
  7.2 1.8 copy-start
  7.2 3.9 copy-start.14
  11.2 5.9 %copy-start.10 = (bf16[128,576]{0,1:T(8,128)(2,1)}, bf16[128,576]{0,1:T(8,128)(2,1)S(1)}, u32[]{:S(2)}) copy-start(bf16[128,576]{0,1:T(8,128)(2,1)S(1)} %pad_maximum_fusion.1) | copy-start | bytes 442372
  17.2 13.5 %copy-start.12 = (s32[128,6]{0,1:T(8,128)S(1)}, s32[128,6]{0,1:T(8,128)}, u32[]{:S(2)}) copy-start(s32[128,6]{0,1:T(8,128)} %param.21) | copy-start | bytes 9220
  17.2 13.9 %copy-start.3 = (bf16[128,2048]{1,0:T(8,128)(2,1)S(1)}, bf16[128,2048]{1,0:T(8,128)(2,1)}, u32[]{:S(2)}) copy-start(bf16[128,2048]{1,0:T(8,128)(2,1)} %param.13) | copy-start | bytes 1572868
  17.2 13.9 %copy-start.8 = (bf16[2048,384]{1,0:T(8,128)(2,1)S(1)}, bf16[2048,384]{1,0:T(8,128)(2,1)}, u32[]{:S(2)}) copy-start(bf16[2048,384]{1,0:T(8,128)(2,1)} %param.15) | copy-start | bytes 4718596
  17.2 221.7 %all-to-all-start = ((bf16[64,128,576]{1,2,0:T(8,128)(2,1)}), bf16[64,128,576]{1,2,0:T(8,128)(2,1)}, u32[]{:S(2)}, u32[]{:S(2)}) async-start(bf16[64,128,576]{1,2,0:T(8,128)(2,1)} %stack.2), calls=%async_computation | async-start | bytes 18874368 | tf_op jit(solution)/shard_map/all_to_all | solution.py:85
  30.6 1.7 copy-start.11
  245.6 3.4 copy-start.2
  260.4 9.2 %copy-start.9 = (bf16[256,2048]{1,0:T(8,128)(2,1)S(1)}, bf16[256,2048]{1,0:T(8,128)(2,1)}, u32[]{:S(2)}) copy-start(bf16[256,2048]{1,0:T(8,128)(2,1)} %param.19) | copy-start | bytes 3145732
  270.8 13.9 %all-to-all-start.1 = ((bf16[4,128,512]{2,1,0:T(8,128)(2,1)}), bf16[4,128,512]{2,1,0:T(8,128)(2,1)S(1)}, u32[]{:S(2)}, u32[]{:S(2)}) async-start(bf16[4,128,512]{2,1,0:T(8,128)(2,1)} %bitcast.130), calls=%async_computation.1 | async-start | bytes 1048576 | tf_op jit(solution)/shard_map/all_to_all | solution.py:124
  274.8 83.0 %all-gather.3.cloned.1.call-start = ((), (), s32[]{:S(2)}) async-start(), calls=%async_computation.9 | async-start | bytes 3932160 | tf_op jit(solution)/shard_map/all_gather | solution.py:156
  284.8 1.1 copy-start.6
  320.8 81.1 %all-gather.5.cloned.1.call-start = ((), (), s32[]{:S(2)}) async-start(), calls=%async_computation.11 | async-start | bytes 3932160 | tf_op jit(solution)/shard_map/all_gather | solution.py:156
  355.4 5.2 copy-start.17
  356.5 89.2 %reduce-scatter.3.cloned.1.call-start = ((), (), s32[]{:S(2)}) async-start(), calls=%async_computation.10 | async-start | bytes 3932160 | tf_op jit(solution)/shard_map/reduce_scatter | solution.py:168
  357.8 2.8 copy-start.5
  360.7 3.9 copy-start.16
  372.7 32.0 %copy-start.15 = (bf16[1,2048,352]{1,2,0:T(8,128)(2,1)S(1)}, bf16[1,2048,352]{1,2,0:T(8,128)(2,1)}, u32[]{:S(2)}) copy-start(bf16[1,2048,352]{1,2,0:T(8,128)(2,1)} %param.23) | copy-start | bytes 4325380
  372.7 115.9 %reduce-scatter.5.cloned.1.call-start = ((), (), s32[]{:S(2)}) async-start(), calls=%async_computation.12 | async-start | bytes 3932160 | tf_op jit(solution)/shard_map/reduce_scatter | solution.py:168
  401.9 2.8 copy-start.4
  447.8 54.2 %copy-start.13 = (f32[128,6]{0,1:T(8,128)S(1)}, f32[128,6]{0,1:T(8,128)}, u32[]{:S(2)}) copy-start(f32[128,6]{0,1:T(8,128)} %param.22) | copy-start | bytes 9220
  447.8 43.1 %all-to-all-start.3 = ((bf16[64,12,512]{2,1,0:T(8,128)(2,1)}), bf16[64,12,512]{2,1,0:T(8,128)(2,1)S(1)}, u32[]{:S(2)}, u32[]{:S(2)}) async-start(bf16[64,12,512]{2,1,0:T(8,128)(2,1)} %reshape.260), calls=%async_computation.4 | async-start | bytes 2097152 | tf_op jit(solution)/shard_map/all_to_all | solution.py:171
  490.8 39.4 %all-to-all-start.5 = ((bf16[64,12,512]{2,1,0:T(8,128)(2,1)}), bf16[64,12,512]{2,1,0:T(8,128)(2,1)}, u32[]{:S(2)}, u32[]{:S(2)}) async-start(bf16[64,12,512]{2,1,0:T(8,128)(2,1)} %reshape.262), calls=%async_computation.7 | async-start | bytes 2097152 | tf_op jit(solution)/shard_map/all_to_all | solution.py:171
  534.9 1.2 copy-start.7
  534.9 15.3 %copy-start.1 = (bf16[2048,576]{0,1:T(8,128)(2,1)S(1)}, bf16[2048,576]{0,1:T(8,128)(2,1)}, u32[]{:S(2)}) copy-start(bf16[2048,576]{0,1:T(8,128)(2,1)} %param.16) | copy-start | bytes 7077892
Sparse Core Ops, SparseCore 0:
  321.0 36.8 all-gather.2
  359.6 42.2 all-gather.4
  404.5 41.1 reduce-scatter.2
  448.0 40.5 reduce-scatter.4
